TPU v7x, 32 devices: a whole 2x2x4 slice. The times are simulated.
32 devices in a mesh: blk: 8 (over z, y), img: 4 (over x, core).
Axes of the slice: x: 2, y: 2, z: 4, core: 2. Of those that a mesh axis runs over, the one named last changes fastest.
Arguments:
- images: bfloat16 [4096, 1152], P(('blk', 'img')), may hold values from -0.1875 to 0.1875
- texts: bfloat16 [4096, 1152], P(('blk', 'img')), may hold values from -0.1875 to 0.1875
- cache: bfloat16 [4096, 1152], P(('blk', 'img')), may hold values from -0.1875 to 0.1875
- mate_owner: int32 [4096, 4], P(('blk', 'img')), may hold values from 0 to 31, all different within a row; in each aligned block of 128 rows (0 to 127, 128 to 255, ...) at most 32 rows name the same one
- mate_row: int32 [4096, 4], P(('blk', 'img')), may hold values from 0 to 127
- mate_count: int32 [4096], P(('blk', 'img')), may hold values from 1 to 4
- log_scale: float32 [1], replicated, may hold values from 1.8 to 2.6
- bias: float32 [1], replicated, may hold values from -6 to -2
Outputs:
- image_grad: float32 [4096, 1152], P(('blk', 'img'))
- text_grad: float32 [4096, 1152], P(('blk', 'img'))
- cache_grad: float32 [4096, 1152], P(('blk', 'img'))
Inputs may be any that keep to these rules, and one draw needn't show every extreme that they name: `mate_owner`: among the 4 entries of the 128 rows of one device, each owner is named at most 32 times, and some device names some owner exactly 32 times; within a row the owners differ.
All inputs are finite; a program needn't handle non-finite values.
Results may differ from a plain program's by a relative error of at most 0.0034.
Values may be sent and summed in bfloat16 or wider, within the bound.
No kernel may reach another device: no remote copies, remote signals or barrier semaphores. Data moves between devices by JAX's collectives and lax.ppermute only.
A program may use at most 128 MiB of HBM per device.

v0:
```python
import jax
import jax.numpy as jnp
from jax import lax
from jax.sharding import PartitionSpec as P


def shards(images, texts, cache, mate_owner, mate_row, mate_count, log_scale, bias):
    scale = jnp.exp(log_scale[0])
    offset = bias[0]
    rows_dev, width = images.shape
    mates = mate_owner.shape[1]
    n_img = lax.axis_size("img")
    n_blk = lax.axis_size("blk")
    owners = n_img * n_blk
    cap = max(2, 2 * rows_dev * mates // owners)
    blk_idx = lax.axis_index("blk")
    img_idx = lax.axis_index("img")
    img_all = lax.all_gather(images, "img", axis=0, tiled=True)
    group_rows = img_all.shape[0]
    group_ids = blk_idx * n_img * rows_dev + jnp.arange(group_rows, dtype=jnp.int32)

    def coefficients(left, right, left_ids, right_ids):
        logits = scale * jnp.dot(left, right.T, preferred_element_type=jnp.float32) + offset
        same = (left_ids[:, None] == right_ids[None, :]).astype(jnp.float32)
        return (scale * (jax.nn.sigmoid(logits) - same)).astype(jnp.bfloat16)

    def column_ids(count):
        where_at = jnp.arange(count, dtype=jnp.int32)
        return (where_at // rows_dev * n_img + img_idx) * rows_dev + where_at % rows_dev

    piece = lax.all_gather(texts, "blk", axis=0, tiled=True)
    coeff = coefficients(img_all, piece, group_ids, column_ids(piece.shape[0]))
    partial_img = jnp.dot(coeff, piece, preferred_element_type=jnp.float32)
    txt_all = lax.all_gather(texts, "img", axis=0, tiled=True)
    piece = lax.all_gather(images, "blk", axis=0, tiled=True)
    coeff = coefficients(txt_all, piece, group_ids, column_ids(piece.shape[0]))
    partial_txt = jnp.dot(coeff, piece, preferred_element_type=jnp.float32)
    text_grad = lax.psum_scatter(partial_txt, "img", scatter_dimension=0, tiled=True)
    image_grad = lax.psum_scatter(partial_img, "img", scatter_dimension=0, tiled=True)
    owner_flat = mate_owner.reshape(-1)
    row_flat = mate_row.reshape(-1)
    owner_hits = (owner_flat[:, None] == jnp.arange(owners, dtype=jnp.int32)[None, :]).astype(
        jnp.int32
    )
    rank = jnp.sum((jnp.cumsum(owner_hits, axis=0) - owner_hits) * owner_hits, axis=1)
    slot = owner_flat * cap + rank
    table = jnp.zeros((owners * cap,), jnp.int32).at[slot].set(row_flat).reshape(owners, cap)
    asked = lax.all_to_all(table, ("blk", "img"), split_axis=0, concat_axis=0, tiled=True)
    served = jnp.take(cache, asked.reshape(-1), axis=0).reshape(owners, cap, width)
    pulled = lax.all_to_all(
        served, ("blk", "img"), split_axis=0, concat_axis=0, tiled=True
    ).reshape(owners * cap, width)
    mate_emb = jnp.take(pulled, slot, axis=0).reshape(rows_dev, mates, width)
    mate_logit = (
        scale * jnp.einsum("rd,rkd->rk", images, mate_emb, preferred_element_type=jnp.float32)
        + offset
    )
    live = jnp.arange(mates, dtype=jnp.int32)[None, :] < mate_count[:, None]
    mate_coeff = jnp.where(live, scale * (jax.nn.sigmoid(mate_logit) - 1.0), 0.0).astype(
        jnp.bfloat16
    )
    slot_hits = slot[:, None] == jnp.arange(owners * cap, dtype=jnp.int32)[None, :]
    spread = jnp.where(slot_hits, mate_coeff.reshape(-1)[:, None].astype(jnp.float32), 0.0)
    weights = jnp.sum(spread.reshape(rows_dev, mates, owners * cap), axis=1).astype(jnp.bfloat16)
    image_grad = image_grad + jnp.dot(weights, pulled, preferred_element_type=jnp.float32)
    slot_grad = lax.dot_general(
        weights, images, (((0,), (0,)), ((), ())), preferred_element_type=jnp.float32
    )
    returned = lax.all_to_all(
        slot_grad.reshape(owners, cap, width),
        ("blk", "img"),
        split_axis=0,
        concat_axis=0,
        tiled=True,
    ).reshape(owners * cap, width)
    cache_rows = cache.shape[0]
    row_hits = (
        asked.reshape(-1)[:, None] == jnp.arange(cache_rows, dtype=jnp.int32)[None, :]
    ).astype(jnp.float32)
    cache_grad = lax.dot_general(
        row_hits,
        returned,
        (((0,), (0,)), ((), ())),
        precision=lax.Precision.HIGHEST,
        preferred_element_type=jnp.float32,
    )
    return (image_grad, text_grad, cache_grad)


def solution(mesh):
    return jax.shard_map(
        shards,
        mesh=mesh,
        in_specs=(
            P(("blk", "img"), None),
            P(("blk", "img"), None),
            P(("blk", "img"), None),
            P(("blk", "img"), None),
            P(("blk", "img"), None),
            P(("blk", "img")),
            P(),
            P(),
        ),
        out_specs=(P(("blk", "img"), None), P(("blk", "img"), None), P(("blk", "img"), None)),
        check_vma=False,
    )
```

profile of v0, /device:TPU:0, one launch (start us, length us, event | category | flops | bytes accessed | tf_op | source)
XLA Modules:
  0.0 319.4 jit_solution(11909137349858240085)
XLA Ops:
  8.0 0.7 all-gather.7.cloned.1.call-update
  8.7 0.8 copy.29
  9.7 1.2 reduce-window.6
  11.1 0.7 broadcast_multiply_fusion
  12.0 0.8 copy.35
  13.0 2.4 scatter_custom_fusion
  15.6 14.3 %all_to_all.19 = s32[32,1,32]{2,1,0:T(1,128)S(1)} all-to-all(s32[32,1,32]{2,1,0:T(1,128)S(1)} %all_to_all.12), channel_id=1, replica_groups=mesh['blk'=8,'img'=4] {'blk','img'}, dimensions={0} | all-to-all | bytes 8192 | tf_op jit(solution)/shard_map/all_to_all | solution.py:48
  30.4 0.7 reduce.7
  31.2 4.2 %gather_fusion = bf16[1024,1152]{1,0:T(8,128)(2,1)S(1)} fusion(bf16[128,1152]{1,0:T(8,128)(2,1)S(1)} %copy-done, s32[1024]{0:T(1024)S(1)} %broadcast_clamp_fusion), kind=kCustom, calls=%fused_computation | custom fusion | bytes 4722688 | tf_op jit(solution)/shard_map/jit(_take)/gather | solution.py:49
  35.4 1.8 broadcast_select_fusion
  37.2 2.9 all-to-all-start.1
  43.1 79.7 %all-to-all-done.1 = bf16[32,32,1152]{2,1,0:T(8,128)(2,1)S(1)} async-done(((bf16[32,32,1152]{2,1,0:T(8,128)(2,1)}), bf16[32,32,1152]{2,1,0:T(8,128)(2,1)S(1)}, u32[]{:S(2)}, u32[]{:S(2)}) %all-to-all-start.1) | async-done | bytes 2359328 | tf_op jit(solution)/shard_map/all_to_all | solution.py:50
  122.8 2.8 gather_fusion.1
  125.7 3.3 %gather.15 = bf16[128,4,1152]{2,1,0:T(4,128)(2,1)} reshape(bf16[512,1152]{1,0:T(8,128)(2,1)} %gather_fusion.1) | data formatting | bytes 2359296 | tf_op jit(solution)/shard_map/jit(_take)/gather | solution.py:53
  129.0 3.4 %fusion.4 = f32[128,1,4]{2,1,0:T(1,128)S(1)} fusion(bf16[128,4,1152]{2,1,0:T(4,128)(2,1)} %gather.15, pred[128,4]{1,0:T(8,128)(4,1)S(1)} %copy.33, bf16[128,1152,1]{1,0,2:T(8,128)(2,1)S(1)} %bitcast.71), kind=kOutput, calls=%fused_computation.13 | convolution fusion | flops 1769472 | bytes 1477120 | tf_op jit(solution)/shard_map/rd,rkd->rk/dot_general | solution.py:55
  132.8 3.0 fusion.48
  135.7 3.7 %all-to-all-start.2 = ((f32[32,32,1152]{2,1,0:T(8,128)}), f32[32,32,1152]{2,1,0:T(8,128)}, u32[]{:S(2)}, u32[]{:S(2)}) async-start(f32[32,32,1152]{2,1,0:T(8,128)} %bitcast.69), calls=%async_computation.4 | async-start | bytes 9437184 | tf_op jit(solution)/shard_map/all_to_all | solution.py:69
  139.5 7.4 %fusion.8 = f32[512,1152]{1,0:T(8,128)} fusion(bf16[1024,1152]{1,0:T(8,128)(2,1)} %all-gather.7.cloned.1.call-done, bf16[512,1152]{1,0:T(8,128)(2,1)} %all-gather.5.cloned.1.call-done, s32[1024]{0:T(1024)S(1)} %fusion.29, f32[]{:T(128)} %bitcast.64, f32[]{:T(128)} %bitcast, s32[512]{0:T(512)S(1)} %iota_add_fusion), kind=kOutput, calls=%fused_computation.17 | convolution fusion | flops 2421161984 | bytes 5904392 | tf_op jit(solution)/shard_map/dot_general | solution.py:33
  147.2 92.1 %all-gather.11.cloned.1.call-done = bf16[1024,1152]{1,0:T(8,128)(2,1)} async-done(((bf16[128,1152]{1,0:T(8,128)(2,1)}), bf16[1024,1152]{1,0:T(8,128)(2,1)}) %all-gather.11.cloned.1.call-update) | async-done | bytes 2359312 | tf_op jit(solution)/shard_map/all_gather | solution.py:35
  239.3 7.3 %fusion.7 = f32[512,1152]{1,0:T(8,128)} fusion(bf16[1024,1152]{1,0:T(8,128)(2,1)} %all-gather.11.cloned.1.call-done, bf16[512,1152]{1,0:T(8,128)(2,1)} %all-gather.9.cloned.1.call-done, s32[1024]{0:T(1024)S(1)} %fusion.29, f32[]{:T(128)} %bitcast.66, f32[]{:T(128)} %bitcast, s32[512]{0:T(512)S(1)} %iota_add_fusion), kind=kOutput, calls=%fused_computation.16 | convolution fusion | flops 2421161984 | bytes 5904392 | tf_op jit(solution)/shard_map/dot_general | solution.py:37
  246.7 30.3 %reduce-scatter.3.cloned.1.call-done = f32[128,1152]{1,0:T(8,128)} async-done(((f32[512,1152]{1,0:T(8,128)}), f32[128,1152]{1,0:T(8,128)}) %reduce-scatter.3.cloned.1.call-update) | async-done | bytes 589840 | tf_op jit(solution)/shard_map/reduce_scatter | solution.py:39
  277.0 2.4 convolution_add_fusion
  279.4 5.1 %fusion.11 = f32[128,1152]{1,0:T(8,128)} fusion(f32[1024,1152]{1,0:T(8,128)} %bitcast.12, s32[1024]{0:T(1024)S(1)} %reshape.194), kind=kOutput, calls=%fused_computation.21 | convolution fusion | flops 1812070400 | bytes 5312512 | tf_op jit(solution)/shard_map/dot_general | solution.py:80
  284.5 28.0 %reduce-scatter.5.cloned.1.call-done = f32[128,1152]{1,0:T(8,128)} async-done(((f32[512,1152]{1,0:T(8,128)}), f32[128,1152]{1,0:T(8,128)}) %reduce-scatter.5.cloned.1.call-update) | async-done | bytes 589840 | tf_op jit(solution)/shard_map/reduce_scatter | solution.py:38
  (51 shorter events, 4.9 us)
Async XLA Ops:
  7.2 24.1 %copy-start = (bf16[128,1152]{1,0:T(8,128)(2,1)S(1)}, bf16[128,1152]{1,0:T(8,128)(2,1)}, u32[]{:S(2)}) copy-start(bf16[128,1152]{1,0:T(8,128)(2,1)} %param.10) | copy-start | bytes 884740
  7.2 132.3 %all-gather.5.cloned.1.call-start = ((), (), s32[]{:S(2)}) async-start(), calls=%async_computation.5 | async-start | bytes 1474560 | tf_op jit(solution)/shard_map/all_gather | solution.py:18
  7.9 131.6 %all-gather.7.cloned.1.call-start = ((), (), s32[]{:S(2)}) async-start(), calls=%async_computation.6 | async-start | bytes 2654208 | tf_op jit(solution)/shard_map/all_gather | solution.py:31
  37.2 4.4 %copy-start.2 = (s32[128,4]{0,1:T(4,128)S(1)}, s32[128,4]{0,1:T(4,128)}, u32[]{:S(2)}) copy-start(s32[128,4]{0,1:T(4,128)} %param.11) | copy-start | bytes 6148
  37.2 85.7 %all-to-all-start.1 = ((bf16[32,32,1152]{2,1,0:T(8,128)(2,1)}), bf16[32,32,1152]{2,1,0:T(8,128)(2,1)S(1)}, u32[]{:S(2)}, u32[]{:S(2)}) async-start(bf16[32,32,1152]{2,1,0:T(8,128)(2,1)} %broadcast_select_fusion), calls=%async_computation.2 | async-start | bytes 4718592 | tf_op jit(solution)/shard_map/all_to_all | solution.py:50
  40.1 107.1 %all-gather.9.cloned.1.call-start = ((), (), s32[]{:S(2)}) async-start(), calls=%async_computation.8 | async-start | bytes 1474560 | tf_op jit(solution)/shard_map/all_gather | solution.py:34
  40.8 198.5 %all-gather.11.cloned.1.call-start = ((), (), s32[]{:S(2)}) async-start(), calls=%async_computation.9 | async-start | bytes 2654208 | tf_op jit(solution)/shard_map/all_gather | solution.py:35
  125.7 3.3 %copy-start.1 = (bf16[128,1152]{1,0:T(8,128)(2,1)S(1)}, bf16[128,1152]{1,0:T(8,128)(2,1)}, u32[]{:S(2)}) copy-start(bf16[128,1152]{1,0:T(8,128)(2,1)} %param.8) | copy-start | bytes 884740
  129.0 3.4 %copy-start.3 = (s32[128]{0:T(128)S(1)}, s32[128]{0:T(128)}, u32[]{:S(2)}) copy-start(s32[128]{0:T(128)} %param.13) | copy-start | bytes 1540
  135.7 143.7 %all-to-all-start.2 = ((f32[32,32,1152]{2,1,0:T(8,128)}), f32[32,32,1152]{2,1,0:T(8,128)}, u32[]{:S(2)}, u32[]{:S(2)}) async-start(f32[32,32,1152]{2,1,0:T(8,128)} %bitcast.69), calls=%async_computation.4 | async-start | bytes 9437184 | tf_op jit(solution)/shard_map/all_to_all | solution.py:69
  139.4 137.6 %reduce-scatter.3.cloned.1.call-start = ((), (), s32[]{:S(2)}) async-start(), calls=%async_computation.7 | async-start | bytes 2949120 | tf_op jit(solution)/shard_map/reduce_scatter | solution.py:39
  146.9 165.6 %reduce-scatter.5.cloned.1.call-start = ((), (), s32[]{:S(2)}) async-start(), calls=%async_computation.10 | async-start | bytes 2949120 | tf_op jit(solution)/shard_map/reduce_scatter | solution.py:38
Sparse Core Ops, SparseCore 0:
  9.5 20.2 all-gather.4
  32.1 85.5 all-gather.6
  119.3 14.3 all-gather.8
  135.7 103.5 all-gather.10
  241.7 35.2 reduce-scatter.2
  280.0 32.5 reduce-scatter.4
where the time goes:
time: 320 us; the launch traced here: 319 us
  waiting for transfers between devices  233 us (73%)
  matrix products  28.6 us (9%)
  local copies, waits for them, and re-layouts  16.2 us (5%)
  between operations  15.6 us (5%)
  blocking collectives  14.3 us (4%)
  starting transfers between devices  6.98 us (2%)
  other arithmetic  4.88 us (2%)
    all_gather x1, waiting for transfers between devices, shards(): piece = lax.all_gather(images, 'blk', axis=0, tiled=True)  92.1 us
    all_to_all x1, waiting for transfers between devices, shards(): lax.all_to_all(served, ('blk', 'img'), split_axis=0, concat_axis=0, tiled...  79.7 us
    reduce_scatter x1, waiting for transfers between devices, shards(): lax.psum_scatter(partial_img, 'img', scatter_dimension=0, tiled=True)  30.3 us
    reduce_scatter x1, waiting for transfers between devices, shards(): lax.psum_scatter(partial_txt, 'img', scatter_dimension=0, tiled=True)  28 us
    all_to_all x1, blocking collectives, shards(): lax.all_to_all(table, ('blk', 'img'), split_axis=0, concat_axis=0, tiled=...  14.3 us
    dot_general x1, matrix products, shards(): partial_img = jnp.dot(coeff, piece, preferred_element_type=jnp.float32)  7.43 us
    dot_general x1, matrix products, shards(): partial_txt = jnp.dot(coeff, piece, preferred_element_type=jnp.float32)  7.33 us
  transfers between devices with their start and end apart: 8, of which 4 were waited for; matrix products, arithmetic and copies ran while one was open for 16% of the time, Pallas kernels for 0%

commit v1 on v0

--- a/solution.py
+++ b/solution.py
@@ -32,7 +32,12 @@
     coeff = coefficients(img_all, piece, group_ids, column_ids(piece.shape[0]))
     partial_img = jnp.dot(coeff, piece, preferred_element_type=jnp.float32)
     txt_all = lax.all_gather(texts, "img", axis=0, tiled=True)
-    piece = lax.all_gather(images, "blk", axis=0, tiled=True)
+    ring = [images]
+    for hop in range(7):
+        ring.append(lax.ppermute(ring[-1], "blk", [(dev, (dev + 1) % 8) for dev in range(8)]))
+    piece = jnp.roll(
+        jnp.concatenate(ring[::-1], axis=0), (lax.axis_index("blk") + 1) * ring[0].shape[0], axis=0
+    )
     coeff = coefficients(txt_all, piece, group_ids, column_ids(piece.shape[0]))
     partial_txt = jnp.dot(coeff, piece, preferred_element_type=jnp.float32)
     text_grad = lax.psum_scatter(partial_txt, "img", scatter_dimension=0, tiled=True)

time: 320 us -> 309 us (0.966)
  waiting for transfers between devices: 233 us -> 198 us
  local copies, waits for them, and re-layouts: 16.2 us -> 37.9 us
  starting transfers between devices: 6.98 us -> 23.9 us
  blocking collectives: 14.3 us -> 0 us
    ppermute x0 -> x7, waiting for transfers between devices: none -> 122 us  [shards(): lax.ppermute(ring[-1], 'blk', [(dev, (dev + 1) % 8) for dev in range(8)])]
    all_gather x1 -> x0, waiting for transfers between devices: 92.1 us -> none  [shards(): piece = lax.all_gather(images, 'blk', axis=0, tiled=True)]
    all_to_all x1, waiting for transfers between devices: 79.7 us -> 0.01 us  [shards(): lax.all_to_all(served, ('blk', 'img'), split_axis=0, concat_axis=0, tiled...]
    all_to_all x1, waiting for transfers between devices: 0.01 us -> 44.5 us  [shards(): lax.all_to_all(slot_grad.reshape(owners, cap, width), ('blk', 'img'), spl...]
    reduce_scatter x1, waiting for transfers between devices: 28 us -> 0.01 us  [shards(): lax.psum_scatter(partial_txt, 'img', scatter_dimension=0, tiled=True)]
    unnamed x10 -> x33, local copies, waits for them, and re-layouts: 1.6 us -> 22 us
    all_to_all x1 -> x0, blocking collectives: 14.3 us -> none  [shards(): lax.all_to_all(table, ('blk', 'img'), split_axis=0, concat_axis=0, tiled=...]
    all_to_all x0 -> x1, starting transfers between devices: none -> 7.33 us  [shards(): lax.all_to_all(table, ('blk', 'img'), split_axis=0, concat_axis=0, tiled=...]
  transfers between devices with their start and end apart: 8 -> 15, of which waited for: 4 -> 9; matrix products, arithmetic and copies ran while one was open for 16% -> 22% of each run, Pallas kernels for 0% -> 0%
where the time goes in v1:
time: 309 us
  waiting for transfers between devices  198 us (64%)
  local copies, waits for them, and re-layouts  37.9 us (12%)
  matrix products  28.4 us (9%)
  starting transfers between devices  23.9 us (8%)
  between operations  15.4 us (5%)
  other arithmetic  4.86 us (2%)
    ppermute x7, waiting for transfers between devices, shards(): lax.ppermute(ring[-1], 'blk', [(dev, (dev + 1) % 8) for dev in range(8)])  122 us
    all_to_all x1, waiting for transfers between devices, shards(): lax.all_to_all(slot_grad.reshape(owners, cap, width), ('blk', 'img'), spl...  44.5 us
    reduce_scatter x1, waiting for transfers between devices, shards(): lax.psum_scatter(partial_img, 'img', scatter_dimension=0, tiled=True)  23.4 us
    unnamed x33, local copies, waits for them, and re-layouts  22 us
    dot_general x1, matrix products, shards(): partial_txt = jnp.dot(coeff, piece, preferred_element_type=jnp.float32)  7.34 us
    all_to_all x1, starting transfers between devices, shards(): lax.all_to_all(table, ('blk', 'img'), split_axis=0, concat_axis=0, tiled=...  7.33 us
    dot_general x1, matrix products, shards(): partial_img = jnp.dot(coeff, piece, preferred_element_type=jnp.float32)  7.24 us
    all_to_all x1, starting transfers between devices, shards(): lax.all_to_all(slot_grad.reshape(owners, cap, width), ('blk', 'img'), spl...  6.83 us
  transfers between devices with their start and end apart: 15, of which 9 were waited for; matrix products, arithmetic and copies ran while one was open for 22% of the time, Pallas kernels for 0%

profile of v1, /device:TPU:0, one launch (start us, length us, event | category | flops | bytes accessed | tf_op | source)
XLA Modules:
  0.0 308.5 jit_solution(10525263864269632808)
XLA Ops:
  12.3 2.4 scatter_custom_fusion
  15.4 7.3 %all-to-all-start = ((s32[32,1,32]{2,1,0:T(1,128)}), s32[32,1,32]{2,1,0:T(1,128)S(1)}, u32[]{:S(2)}, u32[]{:S(2)}) async-start(s32[32,1,32]{2,1,0:T(1,128)} %all_to_all.12), calls=%async_computation.1 | async-start | bytes 32768 | tf_op jit(solution)/shard_map/all_to_all | solution.py:53
  23.5 6.3 %all-to-all-done = s32[32,1,32]{2,1,0:T(1,128)S(1)} async-done(((s32[32,1,32]{2,1,0:T(1,128)}), s32[32,1,32]{2,1,0:T(1,128)S(1)}, u32[]{:S(2)}, u32[]{:S(2)}) %all-to-all-start) | async-done | bytes 4128 | tf_op jit(solution)/shard_map/all_to_all | solution.py:53
  31.2 4.2 %gather_fusion = bf16[1024,1152]{1,0:T(8,128)(2,1)S(1)} fusion(bf16[128,1152]{1,0:T(8,128)(2,1)S(1)} %copy-done, s32[1024]{0:T(1024)S(1)} %broadcast_clamp_fusion), kind=kCustom, calls=%fused_computation | custom fusion | bytes 4722688 | tf_op jit(solution)/shard_map/jit(_take)/gather | solution.py:54
  37.1 2.9 all-to-all-start.1
  41.8 76.5 %collective-permute-done = bf16[128,1152]{1,0:T(8,128)(2,1)S(1)} collective-permute-done((bf16[128,1152]{1,0:T(8,128)(2,1)S(1)}, bf16[128,1152]{1,0:T(8,128)(2,1)S(1)}, u32[]{:S(2)}, u32[]{:S(2)}) %collective-permute-start) | collective-permute-done | bytes 294944 | tf_op jit(solution)/shard_map/ppermute | solution.py:37
  118.3 11.3 %collective-permute-done.1 = bf16[128,1152]{1,0:T(8,128)(2,1)S(1)} collective-permute-done((bf16[128,1152]{1,0:T(8,128)(2,1)S(1)}, bf16[128,1152]{1,0:T(8,128)(2,1)S(1)}, u32[]{:S(2)}, u32[]{:S(2)}) %collective-permute-start.1) | collective-permute-done | bytes 294944 | tf_op jit(solution)/shard_map/ppermute | solution.py:37
  130.3 10.4 %collective-permute-done.2 = bf16[128,1152]{1,0:T(8,128)(2,1)S(1)} collective-permute-done((bf16[128,1152]{1,0:T(8,128)(2,1)S(1)}, bf16[128,1152]{1,0:T(8,128)(2,1)S(1)}, u32[]{:S(2)}, u32[]{:S(2)}) %collective-permute-start.2) | collective-permute-done | bytes 294944 | tf_op jit(solution)/shard_map/ppermute | solution.py:37
  141.4 3.0 collective-permute-start.3
  144.5 6.5 %collective-permute-done.3 = bf16[128,1152]{1,0:T(8,128)(2,1)} collective-permute-done((bf16[128,1152]{1,0:T(8,128)(2,1)S(1)}, bf16[128,1152]{1,0:T(8,128)(2,1)}, u32[]{:S(2)}, u32[]{:S(2)}) %collective-permute-start.3) | collective-permute-done | bytes 294944 | tf_op jit(solution)/shard_map/ppermute | solution.py:37
  154.4 8.0 %collective-permute-done.4 = bf16[128,1152]{1,0:T(8,128)(2,1)} collective-permute-done((bf16[128,1152]{1,0:T(8,128)(2,1)}, bf16[128,1152]{1,0:T(8,128)(2,1)}, u32[]{:S(2)}, u32[]{:S(2)}) %collective-permute-start.4) | collective-permute-done | bytes 294944 | tf_op jit(solution)/shard_map/ppermute | solution.py:37
  162.4 9.7 %collective-permute-done.5 = bf16[128,1152]{1,0:T(8,128)(2,1)} collective-permute-done((bf16[128,1152]{1,0:T(8,128)(2,1)}, bf16[128,1152]{1,0:T(8,128)(2,1)}, u32[]{:S(2)}, u32[]{:S(2)}) %collective-permute-start.5) | collective-permute-done | bytes 294944 | tf_op jit(solution)/shard_map/ppermute | solution.py:37
  172.1 2.8 gather_fusion.1
  174.9 3.2 %gather.15 = bf16[128,4,1152]{2,1,0:T(4,128)(2,1)} reshape(bf16[512,1152]{1,0:T(8,128)(2,1)} %gather_fusion.1) | data formatting | bytes 2359296 | tf_op jit(solution)/shard_map/jit(_take)/gather | solution.py:58
  178.1 3.4 %fusion.10 = f32[128,1,4]{2,1,0:T(1,128)S(1)} fusion(bf16[128,4,1152]{2,1,0:T(4,128)(2,1)} %gather.15, pred[128,4]{1,0:T(8,128)(4,1)S(1)} %copy.35, bf16[128,1152,1]{1,0,2:T(8,128)(2,1)S(1)} %bitcast.73), kind=kOutput, calls=%fused_computation.17 | convolution fusion | flops 1769472 | bytes 1477120 | tf_op jit(solution)/shard_map/rd,rkd->rk/dot_general | solution.py:60
  181.9 3.0 fusion.63
  184.9 6.8 %all-to-all-start.2 = ((f32[32,32,1152]{2,1,0:T(8,128)}), f32[32,32,1152]{2,1,0:T(8,128)}, u32[]{:S(2)}, u32[]{:S(2)}) async-start(f32[32,32,1152]{2,1,0:T(8,128)} %bitcast.71), calls=%async_computation.4 | async-start | bytes 9437184 | tf_op jit(solution)/shard_map/all_to_all | solution.py:74
  191.8 7.2 %fusion.21 = f32[512,1152]{1,0:T(8,128)} fusion(bf16[1024,1152]{1,0:T(8,128)(2,1)} %all-gather.6.cloned.1.call-done, bf16[512,1152]{1,0:T(8,128)(2,1)} %all-gather.4.cloned.1.call-done, s32[1024]{0:T(1024)S(1)} %fusion.42, f32[]{:T(128)} %bitcast.66, f32[]{:T(128)} %bitcast, s32[512]{0:T(512)S(1)} %iota_add_fusion), kind=kOutput, calls=%fused_computation.26 | convolution fusion | flops 2421161984 | bytes 5904392 | tf_op jit(solution)/shard_map/dot_general | solution.py:33
  199.4 1.8 constant_dynamic-update-slice_fusion.15
  219.1 7.3 %fusion.4 = f32[512,1152]{1,0:T(8,128)} fusion(bf16[2048,1152]{1,0:T(8,128)(2,1)} %constant_dynamic-update-slice_fusion, s32[]{:T(128)S(6)} %select_n.99, bf16[512,1152]{1,0:T(8,128)(2,1)} %all-gather.8.cloned.1.call-done, f32[]{:T(128)} %bitcast.68, f32[]{:T(128)} %bitcast, s32[1024]{0:T(1024)S(1)} %fusion.42, s32[512]{0:T(512)S(1)} %iota_add_fusion), kind=kOutput, calls=%fused_computation.13 | convolution fusion | flops 2421161984 | bytes 8266240 | tf_op jit(solution)/shard_map/dot_general | solution.py:42
  226.5 23.4 %reduce-scatter.3.cloned.1.call-done = f32[128,1152]{1,0:T(8,128)} async-done(((f32[512,1152]{1,0:T(8,128)}), f32[128,1152]{1,0:T(8,128)}) %reduce-scatter.3.cloned.1.call-update) | async-done | bytes 589840 | tf_op jit(solution)/shard_map/reduce_scatter | solution.py:44
  249.9 2.4 convolution_add_fusion
  252.3 44.5 %all-to-all-done.2 = f32[32,32,1152]{2,1,0:T(8,128)} async-done(((f32[32,32,1152]{2,1,0:T(8,128)}), f32[32,32,1152]{2,1,0:T(8,128)}, u32[]{:S(2)}, u32[]{:S(2)}) %all-to-all-start.2) | async-done | bytes 4718624 | tf_op jit(solution)/shard_map/all_to_all | solution.py:74
  296.9 5.1 %fusion.24 = f32[128,1152]{1,0:T(8,128)} fusion(f32[1024,1152]{1,0:T(8,128)} %bitcast.13, s32[1024]{0:T(1024)S(1)} %reshape.194), kind=kOutput, calls=%fused_computation.30 | convolution fusion | flops 1812070400 | bytes 5312512 | tf_op jit(solution)/shard_map/dot_general | solution.py:85
  (87 shorter events, 33.5 us)
Async XLA Ops:
  7.2 24.0 %copy-start = (bf16[128,1152]{1,0:T(8,128)(2,1)S(1)}, bf16[128,1152]{1,0:T(8,128)(2,1)}, u32[]{:S(2)}) copy-start(bf16[128,1152]{1,0:T(8,128)(2,1)} %param.10) | copy-start | bytes 884740
  7.2 184.6 %all-gather.4.cloned.1.call-start = ((), (), s32[]{:S(2)}) async-start(), calls=%async_computation.5 | async-start | bytes 1474560 | tf_op jit(solution)/shard_map/all_gather | solution.py:18
  15.4 14.4 %all-to-all-start = ((s32[32,1,32]{2,1,0:T(1,128)}), s32[32,1,32]{2,1,0:T(1,128)S(1)}, u32[]{:S(2)}, u32[]{:S(2)}) async-start(s32[32,1,32]{2,1,0:T(1,128)} %all_to_all.12), calls=%async_computation.1 | async-start | bytes 32768 | tf_op jit(solution)/shard_map/all_to_all | solution.py:53
  22.8 169.1 %all-gather.6.cloned.1.call-start = ((), (), s32[]{:S(2)}) async-start(), calls=%async_computation.6 | async-start | bytes 2654208 | tf_op jit(solution)/shard_map/all_gather | solution.py:31
  37.1 3.0 copy-start.1
  37.1 117.1 %copy-start.6 = (s32[128,4]{0,1:T(4,128)S(1)}, s32[128,4]{0,1:T(4,128)}, u32[]{:S(2)}) copy-start(s32[128,4]{0,1:T(4,128)} %param.11) | copy-start | bytes 6148
  37.1 134.9 %all-to-all-start.1 = ((bf16[32,32,1152]{2,1,0:T(8,128)(2,1)}), bf16[32,32,1152]{2,1,0:T(8,128)(2,1)S(1)}, u32[]{:S(2)}, u32[]{:S(2)}) async-start(bf16[32,32,1152]{2,1,0:T(8,128)(2,1)} %broadcast_select_fusion), calls=%async_computation.2 | async-start | bytes 4718592 | tf_op jit(solution)/shard_map/all_to_all | solution.py:55
  40.0 179.0 %all-gather.8.cloned.1.call-start = ((), (), s32[]{:S(2)}) async-start(), calls=%async_computation.8 | async-start | bytes 1474560 | tf_op jit(solution)/shard_map/all_gather | solution.py:34
  40.1 78.2 %collective-permute-start = (bf16[128,1152]{1,0:T(8,128)(2,1)S(1)}, bf16[128,1152]{1,0:T(8,128)(2,1)S(1)}, u32[]{:S(2)}, u32[]{:S(2)}) collective-permute-start(bf16[128,1152]{1,0:T(8,128)(2,1)S(1)} %copy-done.1), channel_id=1, source_target_pairs={{0,4},{4,8},{8,12},{12,16},{16,20},{20,24},{24,28},{28,0},{1,5},{5... | collective-permute-start | bytes 884744 | tf_op jit(solution)/shard_map/ppermute | solution.py:37
  118.3 11.3 %collective-permute-start.1 = (bf16[128,1152]{1,0:T(8,128)(2,1)S(1)}, bf16[128,1152]{1,0:T(8,128)(2,1)S(1)}, u32[]{:S(2)}, u32[]{:S(2)}) collective-permute-start(bf16[128,1152]{1,0:T(8,128)(2,1)S(1)} %collective-permute-done), channel_id=1, source_target_pairs={{0,4},{4,8},{8,12},{12,16},{16,20},{20,24},{24,28},{28,0},{1,5},{5... | collective-permute-start | bytes 884744 | tf_op jit(solution)/shard_map/ppermute | solution.py:37
  129.6 0.7 copy-start.2
  130.3 10.4 %collective-permute-start.2 = (bf16[128,1152]{1,0:T(8,128)(2,1)S(1)}, bf16[128,1152]{1,0:T(8,128)(2,1)S(1)}, u32[]{:S(2)}, u32[]{:S(2)}) collective-permute-start(bf16[128,1152]{1,0:T(8,128)(2,1)S(1)} %collective-permute-done.1), channel_id=1, source_target_pairs={{0,4},{4,8},{8,12},{12,16},{16,20},{20,24},{24,28},{28,0},{1,5},{5... | collective-permute-start | bytes 884744 | tf_op jit(solution)/shard_map/ppermute | solution.py:37
  140.7 0.7 copy-start.4
  141.4 9.6 %collective-permute-start.3 = (bf16[128,1152]{1,0:T(8,128)(2,1)S(1)}, bf16[128,1152]{1,0:T(8,128)(2,1)}, u32[]{:S(2)}, u32[]{:S(2)}) collective-permute-start(bf16[128,1152]{1,0:T(8,128)(2,1)S(1)} %collective-permute-done.2), channel_id=1, source_target_pairs={{0,4},{4,8},{8,12},{12,16},{16,20},{20,24},{24,28},{28,0},{1,5},{5... | collective-permute-start | bytes 884744 | tf_op jit(solution)/shard_map/ppermute | solution.py:37
  151.0 11.3 %collective-permute-start.4 = (bf16[128,1152]{1,0:T(8,128)(2,1)}, bf16[128,1152]{1,0:T(8,128)(2,1)}, u32[]{:S(2)}, u32[]{:S(2)}) collective-permute-start(bf16[128,1152]{1,0:T(8,128)(2,1)} %collective-permute-done.3), channel_id=1, source_target_pairs={{0,4},{4,8},{8,12},{12,16},{16,20},{20,24},{24,28},{28,0},{1,5},{5... | collective-permute-start | bytes 884744 | tf_op jit(solution)/shard_map/ppermute | solution.py:37
  162.3 9.7 %collective-permute-start.5 = (bf16[128,1152]{1,0:T(8,128)(2,1)}, bf16[128,1152]{1,0:T(8,128)(2,1)}, u32[]{:S(2)}, u32[]{:S(2)}) collective-permute-start(bf16[128,1152]{1,0:T(8,128)(2,1)} %collective-permute-done.4), channel_id=1, source_target_pairs={{0,4},{4,8},{8,12},{12,16},{16,20},{20,24},{24,28},{28,0},{1,5},{5... | collective-permute-start | bytes 884744 | tf_op jit(solution)/shard_map/ppermute | solution.py:37
  172.1 27.3 %collective-permute-start.6 = (bf16[128,1152]{1,0:T(8,128)(2,1)}, bf16[128,1152]{1,0:T(8,128)(2,1)}, u32[]{:S(2)}, u32[]{:S(2)}) collective-permute-start(bf16[128,1152]{1,0:T(8,128)(2,1)} %collective-permute-done.5), channel_id=1, source_target_pairs={{0,4},{4,8},{8,12},{12,16},{16,20},{20,24},{24,28},{28,0},{1,5},{5... | collective-permute-start | bytes 884744 | tf_op jit(solution)/shard_map/ppermute | solution.py:37
  178.1 3.4 %copy-start.7 = (s32[128]{0:T(128)S(1)}, s32[128]{0:T(128)}, u32[]{:S(2)}) copy-start(s32[128]{0:T(128)} %param.13) | copy-start | bytes 1540
  184.9 112.0 %all-to-all-start.2 = ((f32[32,32,1152]{2,1,0:T(8,128)}), f32[32,32,1152]{2,1,0:T(8,128)}, u32[]{:S(2)}, u32[]{:S(2)}) async-start(f32[32,32,1152]{2,1,0:T(8,128)} %bitcast.71), calls=%async_computation.4 | async-start | bytes 9437184 | tf_op jit(solution)/shard_map/all_to_all | solution.py:74
  191.7 58.2 %reduce-scatter.3.cloned.1.call-start = ((), (), s32[]{:S(2)}) async-start(), calls=%async_computation.7 | async-start | bytes 2949120 | tf_op jit(solution)/shard_map/reduce_scatter | solution.py:44
  199.1 102.9 %reduce-scatter.5.cloned.1.call-start = ((), (), s32[]{:S(2)}) async-start(), calls=%async_computation.9 | async-start | bytes 2949120 | tf_op jit(solution)/shard_map/reduce_scatter | solution.py:43
  199.4 6.9 %copy-start.5 = (bf16[128,1152]{1,0:T(8,128)(2,1)S(1)}, bf16[128,1152]{1,0:T(8,128)(2,1)}, u32[]{:S(2)}) copy-start(bf16[128,1152]{1,0:T(8,128)(2,1)} %copy-done.4) | copy-start | bytes 884740
  199.4 7.6 %copy-start.3 = (bf16[128,1152]{1,0:T(8,128)(2,1)S(1)}, bf16[128,1152]{1,0:T(8,128)(2,1)}, u32[]{:S(2)}) copy-start(bf16[128,1152]{1,0:T(8,128)(2,1)} %copy-done.2) | copy-start | bytes 884740
Sparse Core Ops, SparseCore 0:
  9.5 20.2 all-gather.3
  32.1 85.5 all-gather.5
  152.8 22.1 all-gather.7
  199.2 50.6 reduce-scatter.2
  252.9 39.4 reduce-scatter.4
